TPU v7x, 32 devices: a whole 2x2x4 slice. The times are simulated.
32 devices in a mesh: seq: 4 (over x, core), dp: 8 (over z, y).
Axes of the slice: x: 2, y: 2, z: 4, core: 2. Of those that a mesh axis runs over, the one named last changes fastest.
Arguments:
- inputs: bfloat16 [8, 1024, 4096], P('dp', 'seq'), may hold values from -6 to 6
- queries: bfloat16 [8, 1024, 256], P('dp', 'seq'), may hold values from -6 to 6
- keys: bfloat16 [8, 1024, 256], P('dp', 'seq'), may hold values from -6 to 6
- values: bfloat16 [8, 1024, 256], P('dp', 'seq'), may hold values from -6 to 6
- out_grad: bfloat16 [8, 1024, 256], P('dp', 'seq'), may hold values from -6 to 6
Outputs:
- qkv_grad: bfloat16 [8, 1024, 768], P('dp', 'seq')
- weight_grad: float32 [4096, 768], P('dp')
All inputs are finite; a program needn't handle non-finite values.
Results may differ from a plain program's by a relative error of at most 0.014.
Values may be sent and summed in bfloat16 or wider, within the bound.
No kernel may reach another device: no remote copies, remote signals or barrier semaphores. Data moves between devices by JAX's collectives and lax.ppermute only.
A program may use at most 64 MiB of HBM per device.

v0:
```python
import jax
import jax.numpy as jnp
from jax import lax
from jax.sharding import PartitionSpec as P

HS = 128
HEADS = 2


def block_grads(query, key, value, grad_out, prefix, suffix, scale):
    count = query.shape[0]
    causal = jnp.arange(count)[:, None] >= jnp.arange(count)[None, :]
    f32 = jnp.float32
    score_a = jnp.einsum("thd,shd->hts", grad_out, value, preferred_element_type=f32)
    score_a = jnp.where(causal[None], score_a, 0.0).astype(jnp.bfloat16)
    score_b = jnp.einsum("thd,shd->hts", query, key, preferred_element_type=f32)
    score_b = jnp.where(causal[None], score_b, 0.0).astype(jnp.bfloat16)
    grad_q = jnp.einsum("hts,shd->thd", score_a, key, preferred_element_type=f32) + jnp.einsum(
        "thb,hab->tha", grad_out, prefix, preferred_element_type=f32
    )
    grad_k = jnp.einsum("htj,thd->jhd", score_a, query, preferred_element_type=f32) + jnp.einsum(
        "jhb,hab->jha", value, suffix, preferred_element_type=f32
    )
    grad_v = jnp.einsum("htj,thd->jhd", score_b, grad_out, preferred_element_type=f32) + jnp.einsum(
        "jha,hab->jhb", key, suffix, preferred_element_type=f32
    )
    joined = jnp.concatenate([grad_q, grad_k, grad_v], axis=1) * scale
    return joined.reshape(count, -1).astype(jnp.bfloat16)


def on_device(inputs, queries, keys, values, out_grad):
    tokens = queries.shape[1]
    seq_count = lax.axis_size("seq")
    batch_count = lax.axis_size("dp")
    length_all = tokens * seq_count
    scale = 1.0 / jnp.sqrt(jnp.float32(HS * length_all))
    weight_scale = 1.0 / jnp.sqrt(jnp.float32(batch_count * length_all))
    shape = (tokens, HEADS, HS)
    query = queries[0].reshape(shape)
    key = keys[0].reshape(shape)
    value = values[0].reshape(shape)
    grad_out = out_grad[0].reshape(shape)
    kv_state = jnp.einsum("lhi,lhj->hij", key, value, preferred_element_type=jnp.float32).astype(
        jnp.bfloat16
    )
    dq_state = jnp.einsum(
        "lhi,lhj->hij", query, grad_out, preferred_element_type=jnp.float32
    ).astype(jnp.bfloat16)
    stacked = jnp.stack([kv_state, dq_state])[None]
    position = lax.axis_index("seq")
    piece = lax.all_gather(stacked, "seq", axis=0, tiled=True)
    owners = jnp.arange(piece.shape[0])
    lower = (owners < position).astype(jnp.float32)
    higher = (owners > position).astype(jnp.float32)
    wide = piece.astype(jnp.float32)
    prefix = jnp.einsum("n,nhij->hij", lower, wide[:, 0])
    suffix = jnp.einsum("n,nhij->hij", higher, wide[:, 1])
    prefix = prefix.astype(jnp.bfloat16)
    suffix = suffix.astype(jnp.bfloat16)
    grads = block_grads(query, key, value, grad_out, prefix, suffix, scale)
    features = inputs[0]
    rows_here = lax.psum_scatter(
        (
            lax.dot_general(
                features, grads, (((0,), (0,)), ((), ())), preferred_element_type=jnp.float32
            )
            * weight_scale
        ).astype(jnp.bfloat16),
        "dp",
        scatter_dimension=0,
        tiled=True,
    )
    weight_grad = lax.psum(rows_here, "seq").astype(jnp.float32)
    return (grads[None], weight_grad)


def solution(mesh):
    in_specs = (
        P("dp", "seq", None),
        P("dp", "seq", None),
        P("dp", "seq", None),
        P("dp", "seq", None),
        P("dp", "seq", None),
    )
    out_specs = (P("dp", "seq", None), P("dp", None))
    return jax.shard_map(
        on_device, mesh=mesh, in_specs=in_specs, out_specs=out_specs, check_vma=False
    )
```

profile of v0, /device:TPU:0, one launch (start us, length us, event | category | flops | bytes accessed | tf_op | source)
XLA Modules:
  0.0 193.3 jit_solution(12286816662715219097)
XLA Ops:
  7.3 1.1 reshape_squeeze.14
  8.4 0.9 reshape_squeeze.15
  9.3 0.9 reshape_squeeze.13
  10.2 1.0 copy.45
  11.3 0.2 fusion.9
  11.5 0.2 fusion.10
  11.7 8.6 %all-gather = bf16[8,2,128,128]{3,2,1,0:T(8,128)(2,1)S(1)} all-gather(bf16[2,2,128,128]{3,2,1,0:T(8,128)(2,1)S(1)} %pad_maximum_fusion), channel_id=2, replica_groups=mesh['seq'=4,'dp'=8] {'seq'}, dimensions={0}, use_global_device_ids=true | all-gather | bytes 655360 | tf_op jit(solution)/shard_map/all_gather | solution.py:51
  20.4 0.3 fusion.13
  20.7 0.1 copy.42
  20.8 0.2 convolution_bitcast_fusion.3
  21.1 0.2 convolution_bitcast_fusion.2
  21.3 0.3 fusion.2
  21.5 0.3 fusion.15
  21.8 0.2 convolution_bitcast_fusion.4
  22.0 0.2 fusion.7
  22.3 0.2 fusion.6
  22.5 1.2 fusion.8
  23.7 0.1 fusion.11
  23.8 4.5 %fusion = bf16[4096,768]{0,1:T(8,128)(2,1)} fusion(bf16[256,768]{0,1:T(8,128)(2,1)S(1)} %bitcast.58, bf16[1,256,4096]{2,1,0:T(8,128)(2,1)S(1)} %copy-done), kind=kOutput, calls=%fused_computation.1 | convolution fusion | flops 1616904192 | bytes 8781824 | tf_op jit(solution)/shard_map/dot_general | solution.py:64
  28.3 0.0 all-reduce.2.cloned.1.call-start
  28.4 119.3 %reduce-scatter.2.cloned.1.call-done = bf16[512,768]{0,1:T(8,128)(2,1)} async-done(((bf16[4096,768]{0,1:T(8,128)(2,1)}), bf16[512,768]{0,1:T(8,128)(2,1)}) %reduce-scatter.2.cloned.1.call-update) | async-done | bytes 786448 | tf_op jit(solution)/shard_map/reduce_scatter | solution.py:62
  147.7 0.9 copy.35
  148.6 35.2 %all-reduce.2.cloned.1.call-done = bf16[512,768]{0,1:T(8,128)(2,1)} async-done(((bf16[512,768]{0,1:T(8,128)(2,1)}), bf16[512,768]{0,1:T(8,128)(2,1)}) %all-reduce.2.cloned.1.call-update) | async-done | bytes 786448 | tf_op jit(solution)/shard_map/psum | solution.py:73
  183.9 2.5 %copy.36 = f32[512,768]{1,0:T(8,128)} copy(bf16[512,768]{0,1:T(8,128)(2,1)} %all-reduce.2.cloned.1.call-done) | data formatting | bytes 2359296
  (10 shorter events, 0.2 us)
Async XLA Ops:
  7.2 16.7 %copy-start = (bf16[1,256,4096]{2,1,0:T(8,128)(2,1)S(1)}, bf16[1,256,4096]{2,1,0:T(8,128)(2,1)}, u32[]{:S(2)}) copy-start(bf16[1,256,4096]{2,1,0:T(8,128)(2,1)} %param.5) | copy-start | bytes 6291460
  7.2 140.5 %reduce-scatter.2.cloned.1.call-start = ((), (), s32[]{:S(2)}) async-start(), calls=%async_computation.1 | async-start | bytes 7077888 | tf_op jit(solution)/shard_map/reduce_scatter | solution.py:62
  7.3 14.7 %copy-start.1 = (pred[256,256]{1,0:T(8,128)(4,1)}, pred[256,256]{1,0:T(8,128)(4,1)S(1)}, u32[]{:S(2)}) copy-start(pred[256,256]{1,0:T(8,128)(4,1)S(1)} %iota_compare_fusion) | copy-start | bytes 196612
  28.3 155.6 %all-reduce.2.cloned.1.call-start = ((), (), s32[]{:S(2)}) async-start(), calls=%async_computation.2 | async-start | bytes 1572864 | tf_op jit(solution)/shard_map/psum | solution.py:73
Sparse Core Ops, SparseCore 0:
  28.4 119.2 reduce-scatter.1
  150.1 33.7 all-reduce.1
where the time goes:
time: 194 us; the launch traced here: 193 us
  waiting for transfers between devices  155 us (80%)
  between operations  14.2 us (7%)
  blocking collectives  8.62 us (4%)
  matrix products  8.03 us (4%)
  local copies, waits for them, and re-layouts  7.61 us (4%)
    reduce_scatter x1, waiting for transfers between devices, on_device(): lax.psum_scatter((lax.dot_general(features, grads, (((0,), (0,)), ((), ()...  119 us
    psum x1, waiting for transfers between devices, on_device(): weight_grad = lax.psum(rows_here, 'seq').astype(jnp.float32)  35.2 us
    all_gather x1, blocking collectives, on_device(): piece = lax.all_gather(stacked, 'seq', axis=0, tiled=True)  8.62 us
    dot_general x1, matrix products, on_device(): lax.dot_general(features, grads, (((0,), (0,)), ((), ())), preferred_elem...  4.45 us
  transfers between devices with their start and end apart: 2, of which 2 were waited for; matrix products, arithmetic and copies ran while one was open for 0% of the time, Pallas kernels for 0%

commit v1 on v0

--- a/solution.py
+++ b/solution.py
@@ -48,7 +48,13 @@
     ).astype(jnp.bfloat16)
     stacked = jnp.stack([kv_state, dq_state])[None]
     position = lax.axis_index("seq")
-    piece = lax.all_gather(stacked, "seq", axis=0, tiled=True)
+    n_dev = lax.axis_size("seq")
+    held, blocks = (stacked, [stacked])
+    for _ in range(n_dev - 1):
+        held = lax.ppermute(held, "seq", [(i, (i + 1) % n_dev) for i in range(n_dev)])
+        blocks.insert(0, held)
+    row_of_blocks = jnp.concatenate(blocks, axis=0)
+    piece = jnp.roll(row_of_blocks, (lax.axis_index("seq") + 1) * stacked.shape[0], axis=0)
     owners = jnp.arange(piece.shape[0])
     lower = (owners < position).astype(jnp.float32)
     higher = (owners > position).astype(jnp.float32)

time: 194 us -> 201 us (1.036)
  waiting for transfers between devices: 155 us -> 169 us
  blocking collectives: 8.62 us -> 0 us
    ppermute x0 -> x3, waiting for transfers between devices: none -> 13.1 us  [on_device(): lax.ppermute(held, 'seq', [(i, (i + 1) % n_dev) for i in range(n_dev)])]
    all_gather x1 -> x0, blocking collectives: 8.62 us -> none  [on_device(): piece = lax.all_gather(stacked, 'seq', axis=0, tiled=True)]
  transfers between devices with their start and end apart: 2 -> 5, of which waited for: 2 -> 5; matrix products, arithmetic and copies ran while one was open for 0% -> 1% of each run, Pallas kernels for 0% -> 0%
where the time goes in v1:
time: 201 us; the launch traced here: 200 us
  waiting for transfers between devices  169 us (84%)
  between operations  14.2 us (7%)
  matrix products  8.84 us (4%)
  local copies, waits for them, and re-layouts  7.73 us (4%)
    reduce_scatter x1, waiting for transfers between devices, on_device(): lax.psum_scatter((lax.dot_general(features, grads, (((0,), (0,)), ((), ()...  121 us
    psum x1, waiting for transfers between devices, on_device(): weight_grad = lax.psum(rows_here, 'seq').astype(jnp.float32)  35.2 us
    ppermute x3, waiting for transfers between devices, on_device(): lax.ppermute(held, 'seq', [(i, (i + 1) % n_dev) for i in range(n_dev)])  13.1 us
    dot_general x1, matrix products, on_device(): lax.dot_general(features, grads, (((0,), (0,)), ((), ())), preferred_elem...  4.46 us
  transfers between devices with their start and end apart: 5, of which 5 were waited for; matrix products, arithmetic and copies ran while one was open for 1% of the time, Pallas kernels for 0%

profile of v1, /device:TPU:0, one launch (start us, length us, event | category | flops | bytes accessed | tf_op | source)
XLA Modules:
  0.0 200.4 jit_solution(5762002566043930431)
XLA Ops:
  7.2 1.1 reshape_squeeze.14
  8.3 0.9 reshape_squeeze.15
  9.2 0.9 reshape_squeeze.13
  10.2 1.0 copy.30
  11.2 0.2 fusion.9
  11.4 0.2 fusion.10
  11.7 0.5 collective-permute-start
  12.2 4.6 %collective-permute-done = bf16[1,2,2,128,128]{4,3,2,1,0:T(8,128)(2,1)S(1)} collective-permute-done((bf16[1,2,2,128,128]{4,3,2,1,0:T(8,128)(2,1)S(1)}, bf16[1,2,2,128,128]{4,3,2,1,0:T(8,128)(2,1)S(1)}, u32[]{:S(2)}, u32[]{:S(2)}) %collective-permute-start) | collective-permute-done | bytes 131104 | tf_op jit(solution)/shard_map/ppermute | solution.py:54
  16.8 4.4 %collective-permute-done.1 = bf16[1,2,2,128,128]{4,3,2,1,0:T(8,128)(2,1)S(1)} collective-permute-done((bf16[1,2,2,128,128]{4,3,2,1,0:T(8,128)(2,1)S(1)}, bf16[1,2,2,128,128]{4,3,2,1,0:T(8,128)(2,1)S(1)}, u32[]{:S(2)}, u32[]{:S(2)}) %collective-permute-start.1) | collective-permute-done | bytes 131104 | tf_op jit(solution)/shard_map/ppermute | solution.py:54
  21.2 0.3 fusion.2
  21.4 4.1 %collective-permute-done.2 = bf16[1,2,2,128,128]{4,3,2,1,0:T(8,128)(2,1)S(1)} collective-permute-done((bf16[1,2,2,128,128]{4,3,2,1,0:T(8,128)(2,1)S(1)}, bf16[1,2,2,128,128]{4,3,2,1,0:T(8,128)(2,1)S(1)}, u32[]{:S(2)}, u32[]{:S(2)}) %collective-permute-start.2) | collective-permute-done | bytes 131104 | tf_op jit(solution)/shard_map/ppermute | solution.py:54
  25.8 0.3 fusion.13
  26.2 0.2 convolution_bitcast_fusion.3
  26.5 0.9 convolution_bitcast_fusion.2
  27.4 0.3 fusion.15
  27.7 0.2 convolution_bitcast_fusion.4
  27.8 0.2 fusion.7
  28.1 0.2 fusion.6
  28.3 1.3 fusion.8
  29.8 4.5 %fusion = bf16[4096,768]{0,1:T(8,128)(2,1)} fusion(bf16[256,768]{0,1:T(8,128)(2,1)S(1)} %bitcast.63, bf16[1,256,4096]{2,1,0:T(8,128)(2,1)S(1)} %copy-done), kind=kOutput, calls=%fused_computation.1 | convolution fusion | flops 1616904192 | bytes 8781824 | tf_op jit(solution)/shard_map/dot_general | solution.py:70
  34.3 120.5 %reduce-scatter.2.cloned.1.call-done = bf16[512,768]{0,1:T(8,128)(2,1)} async-done(((bf16[4096,768]{0,1:T(8,128)(2,1)}), bf16[512,768]{0,1:T(8,128)(2,1)}) %reduce-scatter.2.cloned.1.call-update) | async-done | bytes 786448 | tf_op jit(solution)/shard_map/reduce_scatter | solution.py:68
  154.8 0.9 copy.20
  155.8 35.2 %all-reduce.2.cloned.1.call-done = bf16[512,768]{0,1:T(8,128)(2,1)} async-done(((bf16[512,768]{0,1:T(8,128)(2,1)}), bf16[512,768]{0,1:T(8,128)(2,1)}) %all-reduce.2.cloned.1.call-update) | async-done | bytes 786448 | tf_op jit(solution)/shard_map/psum | solution.py:79
  191.0 2.5 %copy.21 = f32[512,768]{1,0:T(8,128)} copy(bf16[512,768]{0,1:T(8,128)(2,1)} %all-reduce.2.cloned.1.call-done) | data formatting | bytes 2359296
  (21 shorter events, 0.6 us)
Async XLA Ops:
  7.2 22.6 %copy-start = (bf16[1,256,4096]{2,1,0:T(8,128)(2,1)S(1)}, bf16[1,256,4096]{2,1,0:T(8,128)(2,1)}, u32[]{:S(2)}) copy-start(bf16[1,256,4096]{2,1,0:T(8,128)(2,1)} %param.5) | copy-start | bytes 6291460
  7.2 147.6 %reduce-scatter.2.cloned.1.call-start = ((), (), s32[]{:S(2)}) async-start(), calls=%async_computation.1 | async-start | bytes 7077888 | tf_op jit(solution)/shard_map/reduce_scatter | solution.py:68
  11.7 5.1 %collective-permute-start = (bf16[1,2,2,128,128]{4,3,2,1,0:T(8,128)(2,1)S(1)}, bf16[1,2,2,128,128]{4,3,2,1,0:T(8,128)(2,1)S(1)}, u32[]{:S(2)}, u32[]{:S(2)}) collective-permute-start(bf16[1,2,2,128,128]{4,3,2,1,0:T(8,128)(2,1)S(1)} %maximum_bitcast_fusion), channel_id=1, source_target_pairs={{0,8},{8,16},{16,24},{24,0},{1,9},{9,17},{17,25},{25,1},{2,10},{10... | collective-permute-start | bytes 393224 | tf_op jit(solution)/shard_map/ppermute | solution.py:54
  16.8 4.4 %collective-permute-start.1 = (bf16[1,2,2,128,128]{4,3,2,1,0:T(8,128)(2,1)S(1)}, bf16[1,2,2,128,128]{4,3,2,1,0:T(8,128)(2,1)S(1)}, u32[]{:S(2)}, u32[]{:S(2)}) collective-permute-start(bf16[1,2,2,128,128]{4,3,2,1,0:T(8,128)(2,1)S(1)} %collective-permute-done), channel_id=1, source_target_pairs={{0,8},{8,16},{16,24},{24,0},{1,9},{9,17},{17,25},{25,1},{2,10},{10... | collective-permute-start | bytes 393224 | tf_op jit(solution)/shard_map/ppermute | solution.py:54
  21.2 4.4 %collective-permute-start.2 = (bf16[1,2,2,128,128]{4,3,2,1,0:T(8,128)(2,1)S(1)}, bf16[1,2,2,128,128]{4,3,2,1,0:T(8,128)(2,1)S(1)}, u32[]{:S(2)}, u32[]{:S(2)}) collective-permute-start(bf16[1,2,2,128,128]{4,3,2,1,0:T(8,128)(2,1)S(1)} %collective-permute-done.1), channel_id=1, source_target_pairs={{0,8},{8,16},{16,24},{24,0},{1,9},{9,17},{17,25},{25,1},{2,10},{10... | collective-permute-start | bytes 393224 | tf_op jit(solution)/shard_map/ppermute | solution.py:54
  34.2 156.8 %all-reduce.2.cloned.1.call-start = ((), (), s32[]{:S(2)}) async-start(), calls=%async_computation.2 | async-start | bytes 1572864 | tf_op jit(solution)/shard_map/psum | solution.py:79
Sparse Core Ops, SparseCore 0:
  34.4 120.4 reduce-scatter.1
  157.2 33.7 all-reduce.1
